TPU v7x, 32 devices: a whole 2x2x4 slice. The times are simulated.
32 devices in a mesh: dp: 8 (over z, core), chan: 4 (over y, x).
Axes of the slice: x: 2, y: 2, z: 4, core: 2. Of those that a mesh axis runs over, the one named last changes fastest.
Arguments:
- images: bfloat16 [16, 16, 16, 2816], P('dp', None, None, 'chan'), may hold values from -6 to 6
- kernel: float32 [7, 7, 2816], P(None, None, 'chan'), may hold values from -0.875 to 0.875
- layernorm_gain: float32 [2816], P('chan'), may hold values from 0.25 to 1.75
- layernorm_bias: float32 [2816], P('chan'), may hold values from -3 to 3
- w_expand: bfloat16 [2816, 11264], P('dp', 'chan'), may hold values from -0.109375 to 0.109375
- w_reduce: bfloat16 [11264, 2816], P('chan', 'dp'), may hold values from -0.0546875 to 0.0546875
- layer_scale: float32 [2816], P('chan'), may hold values from 0.25 to 1
- cotangent: bfloat16 [16, 16, 16, 2816], P('dp', None, None, 'chan'), may hold values from -6 to 6
Outputs:
- output: bfloat16 [16, 16, 16, 2816], P('dp', None, None, 'chan')
- grad_images: bfloat16 [16, 16, 16, 2816], P('dp', None, None, 'chan')
- grad_kernel: float32 [7, 7, 2816], P(None, None, 'chan')
- gain_gradient: float32 [2816], P('chan')
- grad_bias: float32 [2816], P('chan')
- grad_expand: float32 [2816, 11264], P('dp', 'chan')
- grad_reduce: float32 [11264, 2816], P('chan', 'dp')
- grad_scale: float32 [2816], P('chan')
All inputs are finite; a program needn't handle non-finite values.
Results may differ from a plain program's by a relative error of at most 0.025.
Values may be sent and summed in bfloat16 or wider, within the bound.
A program may use at most 128 MiB of HBM per device.

v0:
```python
import math
import jax
import jax.numpy as jnp
from jax import lax
from jax.sharding import PartitionSpec as P

eps = 1e-06


def depthwise(field, kern):
    height = field.shape[1]
    breadth = field.shape[2]
    padded = jnp.pad(field, ((0, 0), (3, 3), (3, 3), (0, 0)))
    total = jnp.zeros(field.shape, jnp.float32)
    for i in range(7):
        for j in range(7):
            total = total + padded[:, i : i + height, j : j + breadth, :] * kern[i, j]
    return total


def normal_cdf(value):
    return 0.5 * (1.0 + jax.scipy.special.erf(value / math.sqrt(2.0)))


def body(
    images, kernel, layernorm_gain, layernorm_bias, w_expand, w_reduce, layer_scale, cotangent
):
    shape_in = images.shape
    height = shape_in[1]
    breadth = shape_in[2]
    positions = shape_in[0] * height * breadth
    local_chan = shape_in[3]
    image_width = local_chan * lax.axis_size("chan")
    xf = images.astype(jnp.float32)
    conv = depthwise(xf, kernel).reshape(positions, local_chan)
    mean_val = lax.psum(jnp.sum(conv, axis=1), "chan")[:, None] / image_width
    centred_rows = conv - mean_val
    var = lax.psum(jnp.sum(centred_rows * centred_rows, axis=1), "chan")[:, None] / image_width
    inverse_deviation = lax.rsqrt(var + eps)
    standardized_input = centred_rows * inverse_deviation
    normed_output = (standardized_input * layernorm_gain + layernorm_bias).astype(jnp.bfloat16)
    normed_all = lax.all_gather(normed_output, "chan", axis=1, tiled=True)
    expand_all = lax.all_gather(w_expand, "dp", axis=0, tiled=True)
    pre = jnp.dot(normed_all, expand_all, preferred_element_type=jnp.float32)
    hidden = (pre * normal_cdf(pre)).astype(jnp.bfloat16)
    reduce_all = lax.all_gather(w_reduce, "dp", axis=1, tiled=True)
    partial_branch = jnp.dot(hidden, reduce_all, preferred_element_type=jnp.float32)
    branch = lax.psum_scatter(
        partial_branch.astype(jnp.bfloat16), "chan", scatter_dimension=1, tiled=True
    ).astype(jnp.float32)
    xr = xf.reshape(positions, local_chan)
    output = (xr + layer_scale * branch).astype(jnp.bfloat16).reshape(shape_in)
    dyf = cotangent.astype(jnp.float32).reshape(positions, local_chan)
    scale_part = jnp.sum(dyf * branch, axis=0)
    dbranch = (dyf * layer_scale).astype(jnp.bfloat16)
    dbranch_all = lax.all_gather(dbranch, "chan", axis=1, tiled=True)
    dhidden = lax.dot_general(
        dbranch_all, reduce_all, (((1,), (1,)), ((), ())), preferred_element_type=jnp.float32
    )
    slope = normal_cdf(pre) + pre * jnp.exp(-0.5 * pre * pre) / math.sqrt(2.0 * math.pi)
    dpre = (dhidden * slope).astype(jnp.bfloat16)
    columns = normed_all
    grad_expand = lax.psum_scatter(
        lax.dot_general(
            columns, dpre, (((0,), (0,)), ((), ())), preferred_element_type=jnp.float32
        ).astype(jnp.bfloat16),
        "dp",
        scatter_dimension=0,
        tiled=True,
    ).astype(jnp.float32)
    partial_normed = lax.dot_general(
        dpre, expand_all, (((1,), (1,)), ((), ())), preferred_element_type=jnp.float32
    )
    normed_grad = lax.psum_scatter(
        partial_normed.astype(jnp.bfloat16), "chan", scatter_dimension=1, tiled=True
    ).astype(jnp.float32)
    columns = dbranch_all
    grad_reduce = (
        lax.psum_scatter(
            lax.dot_general(
                columns, hidden, (((0,), (0,)), ((), ())), preferred_element_type=jnp.float32
            ).astype(jnp.bfloat16),
            "dp",
            scatter_dimension=0,
            tiled=True,
        )
        .astype(jnp.float32)
        .T
    )
    gain_partial = jnp.sum(normed_grad * standardized_input, axis=0)
    bias_part = jnp.sum(normed_grad, axis=0)
    standardized_grad = normed_grad * layernorm_gain
    first_half, second_half = lax.psum(
        (
            jnp.sum(standardized_grad, axis=1),
            jnp.sum(standardized_grad * standardized_input, axis=1),
        ),
        "chan",
    )
    conv_output_grad = inverse_deviation * (
        standardized_grad
        - first_half[:, None] / image_width
        - standardized_input * (second_half[:, None] / image_width)
    )
    conv_output_grad = conv_output_grad.reshape(shape_in)
    padded = jnp.pad(xf, ((0, 0), (3, 3), (3, 3), (0, 0)))
    dpad = jnp.pad(conv_output_grad, ((0, 0), (3, 3), (3, 3), (0, 0)))
    back = cotangent.astype(jnp.float32)
    kern_rows = []
    for i in range(7):
        tap_row = []
        for j in range(7):
            tap_row.append(
                jnp.sum(
                    padded[:, i : i + height, j : j + breadth, :] * conv_output_grad, axis=(0, 1, 2)
                )
            )
            back = back + dpad[:, 6 - i : 6 - i + height, 6 - j : 6 - j + breadth, :] * kernel[i, j]
        kern_rows.append(jnp.stack(tap_row))
    kernel_part = jnp.stack(kern_rows)
    grad_images = back.astype(jnp.bfloat16)
    grad_kernel, gain_gradient, grad_bias, grad_scale = (
        lax.psum(kernel_part.astype(jnp.bfloat16), "dp").astype(jnp.float32),
        lax.psum(gain_partial.astype(jnp.bfloat16), "dp").astype(jnp.float32),
        lax.psum(bias_part.astype(jnp.bfloat16), "dp").astype(jnp.float32),
        lax.psum(scale_part.astype(jnp.bfloat16), "dp").astype(jnp.float32),
    )
    return (
        output,
        grad_images,
        grad_kernel,
        gain_gradient,
        grad_bias,
        grad_expand,
        grad_reduce,
        grad_scale,
    )


def solution(mesh):
    in_specs = (
        P("dp", None, None, "chan"),
        P(None, None, "chan"),
        P("chan"),
        P("chan"),
        P("dp", "chan"),
        P("chan", "dp"),
        P("chan"),
        P("dp", None, None, "chan"),
    )
    out_specs = (
        P("dp", None, None, "chan"),
        P("dp", None, None, "chan"),
        P(None, None, "chan"),
        P("chan"),
        P("chan"),
        P("dp", "chan"),
        P("chan", "dp"),
        P("chan"),
    )
    return jax.shard_map(body, mesh=mesh, in_specs=in_specs, out_specs=out_specs, check_vma=False)
```

profile of v0, /device:TPU:0, one launch (start us, length us, event | category | flops | bytes accessed | tf_op | source)
XLA Modules:
  0.0 969.2 jit_solution(17701858807250672959)
XLA Ops:
  7.2 0.0 all-gather.5.cloned.1.call-start
  7.2 1.2 slice_reduce_fusion.46
  8.4 1.4 slice_reduce_fusion.48
  9.7 1.4 slice_reduce_fusion.47
  11.2 1.3 convert_element_type.71
  12.5 12.3 %fusion.114 = (f32[2,16,16]{2,1,0:T(8,128)S(1)}, f32[2,16,16,704]{3,2,1,0:T(8,128)S(1)}) fusion(f32[704]{0:T(1024)S(1)} %get-tuple-element.115, f32[704]{0:T(1024)S(1)} %get-tuple-element.116, f32[704]{0:T(1024)S(1)} %get-tuple-element.69, f32[704]{0:T(1024)S(1)} %get-tuple-element.70, f32[704]{0:T(1024)S(1)} %get-tuple-element.71, ...), kind=kLoop, calls=%fused_computation.336 | loop fusion | flops 35323392 | bytes 3023616 | tf_op jit(solution)/shard_map/reduce_sum | solution.py:36
  24.8 0.1 reduce_sum.512
  24.9 11.3 %psum.56 = f32[512]{0:T(512)S(1)} all-reduce(f32[512]{0:T(512)S(1)} %reduce_sum.512), channel_id=1, replica_groups=mesh['dp'=8,'chan'=4] {'chan'}, use_global_device_ids=true, to_apply=%region_1.2 | all-reduce | flops 512 | bytes 4096 | tf_op jit(solution)/shard_map/psum | solution.py:36
  36.2 0.1 sub.28
  36.3 0.3 multiply_reduce_fusion.49
  36.7 0.1 reduce_sum.514
  36.7 8.0 psum.57
  44.7 1.9 copy.71
  46.6 1.1 add_convert_fusion
  47.7 0.0 all-gather.5.cloned.1.call-update
  47.7 0.0 all-gather.7.cloned.1.call-start
  47.8 0.7 all-gather.7.cloned.1.call-update
  48.5 0.0 all-gather.9.cloned.1.call-start
  48.5 0.7 all-gather.9.cloned.1.call-update
  49.2 0.3 reduce-scatter.5.cloned.1.call-start
  49.6 40.4 %all-gather.5.cloned.1.call-done = bf16[512,2816]{0,1:T(8,128)(2,1)} async-done(((bf16[512,704]{0,1:T(8,128)(2,1)}), bf16[512,2816]{0,1:T(8,128)(2,1)}) %all-gather.5.cloned.1.call-update) | async-done | bytes 2883600 | tf_op jit(solution)/shard_map/all_gather | solution.py:42
  90.0 145.3 %all-gather.7.cloned.1.call-done = bf16[2816,2816]{1,0:T(8,128)(2,1)} async-done(((bf16[352,2816]{1,0:T(8,128)(2,1)}), bf16[2816,2816]{1,0:T(8,128)(2,1)}) %all-gather.7.cloned.1.call-update) | async-done | bytes 15859728 | tf_op jit(solution)/shard_map/all_gather | solution.py:43
  235.3 15.1 %fusion.115 = f32[512,2816]{1,0:T(8,128)} fusion(bf16[512,2816]{0,1:T(8,128)(2,1)} %all-gather.5.cloned.1.call-done, bf16[2816,2816]{1,0:T(8,128)(2,1)} %all-gather.7.cloned.1.call-done), kind=kOutput, calls=%fused_computation.337 | convolution fusion | flops 8120172544 | bytes 24510464 | tf_op jit(solution)/shard_map/dot_general | solution.py:44
  250.3 128.5 %all-gather.9.cloned.1.call-done = bf16[2816,2816]{0,1:T(8,128)(2,1)} async-done(((bf16[2816,352]{0,1:T(8,128)(2,1)}), bf16[2816,2816]{0,1:T(8,128)(2,1)}) %all-gather.9.cloned.1.call-update) | async-done | bytes 15859728 | tf_op jit(solution)/shard_map/all_gather | solution.py:46
  378.8 16.3 %convolution_convert_fusion.3 = bf16[512,2816]{0,1:T(8,128)(2,1)} fusion(bf16[2816,2816]{0,1:T(8,128)(2,1)} %all-gather.9.cloned.1.call-done, f32[512,2816]{1,0:T(8,128)} %fusion.115), kind=kOutput, calls=%fused_computation.108 | convolution fusion | flops 8128823296 | bytes 24510464 | tf_op jit(solution)/shard_map/dot_general | solution.py:47
  395.1 0.0 reduce-scatter.5.cloned.1.call-update
  395.1 0.0 all-gather.11.cloned.1.call-start
  395.1 2.5 copy.74
  397.6 1.6 copy.72
  399.3 36.0 %reduce-scatter.5.cloned.1.call-done = bf16[512,704]{0,1:T(8,128)(2,1)} async-done(((bf16[512,2816]{0,1:T(8,128)(2,1)}), bf16[512,704]{0,1:T(8,128)(2,1)}) %reduce-scatter.5.cloned.1.call-update) | async-done | bytes 720912 | tf_op jit(solution)/shard_map/reduce_scatter | solution.py:48
  435.3 3.5 fusion.109
  438.8 0.6 reduce-scatter.7.cloned.1.call-start
  439.4 41.4 %all-gather.11.cloned.1.call-done = bf16[512,2816]{0,1:T(8,128)(2,1)} async-done(((bf16[512,704]{0,1:T(8,128)(2,1)}), bf16[512,2816]{0,1:T(8,128)(2,1)}) %all-gather.11.cloned.1.call-update) | async-done | bytes 2883600 | tf_op jit(solution)/shard_map/all_gather | solution.py:56
  480.7 16.0 %fusion.5 = bf16[512,2816]{1,0:T(8,128)(2,1)S(1)} fusion(f32[512,2816]{1,0:T(8,128)} %fusion.115, bf16[512,2816]{0,1:T(8,128)(2,1)} %all-gather.11.cloned.1.call-done, bf16[2816,2816]{0,1:T(8,128)(2,1)} %all-gather.9.cloned.1.call-done), kind=kOutput, calls=%fused_computation.104 | convolution fusion | flops 8134590464 | bytes 27394048 | tf_op jit(solution)/shard_map/dot_general | solution.py:57
  496.8 1.6 copy-done.7
  498.3 13.0 %convolution_convert_fusion.2 = bf16[512,2816]{0,1:T(8,128)(2,1)} fusion(bf16[512,2816]{1,0:T(8,128)(2,1)S(1)} %fusion.5, bf16[2816,2816]{1,0:T(8,128)(2,1)} %all-gather.7.cloned.1.call-done), kind=kOutput, calls=%fused_computation.107 | convolution fusion | flops 8121614336 | bytes 21626880 | tf_op jit(solution)/shard_map/dot_general | solution.py:71
  511.4 0.0 all-reduce.6.cloned.1.call-start
  511.4 41.9 %reduce-scatter.7.cloned.1.call-done = bf16[512,704]{0,1:T(8,128)(2,1)} async-done(((bf16[512,2816]{0,1:T(8,128)(2,1)}), bf16[512,704]{0,1:T(8,128)(2,1)}) %reduce-scatter.7.cloned.1.call-update) | async-done | bytes 720912 | tf_op jit(solution)/shard_map/reduce_scatter | solution.py:74
  553.3 1.7 fusion.113
  555.0 9.1 all-reduce.2
  564.1 2.6 fusion.111
  566.8 1.8 copy.75
  568.6 3.8 multiply_reduce_fusion.2
  572.4 4.2 multiply_reduce_fusion
  576.7 4.5 multiply_reduce_fusion.1
  582.2 0.6 copy-done.3
  582.8 0.0 all-reduce.6.cloned.1.call-update
  582.9 0.0 reduce-scatter.11.cloned.1.call-start
  582.9 15.4 %convolution_convert_fusion = bf16[2816,2816]{1,0:T(8,128)(2,1)} fusion(bf16[512,2816]{0,1:T(8,128)(2,1)} %all-gather.11.cloned.1.call-done, f32[512,2816]{1,0:T(8,128)} %fusion.115), kind=kOutput, calls=%fused_computation.96 | convolution fusion | flops 8135311360 | bytes 24510464 | tf_op jit(solution)/shard_map/dot_general | solution.py:80
  598.4 0.3 reduce-scatter.9.cloned.1.call-start
  598.6 13.9 %convolution_convert_fusion.1 = bf16[2816,2816]{1,0:T(8,128)(2,1)} fusion(bf16[512,2816]{0,1:T(8,128)(2,1)} %all-gather.5.cloned.1.call-done, bf16[512,2816]{1,0:T(8,128)(2,1)} %copy-done.7), kind=kOutput, calls=%fused_computation.97 | convolution fusion | flops 8128102400 | bytes 21626880 | tf_op jit(solution)/shard_map/dot_general | solution.py:64
  612.5 0.0 reduce-scatter.9.cloned.1.call-update
  612.6 2.4 copy.73
  615.0 0.2 reduce_sum.567
  615.2 14.6 %all-reduce.3 = (bf16[704]{0:T(1024)(128)(2,1)S(1)}, bf16[704]{0:T(1024)(128)(2,1)S(1)}, bf16[704]{0:T(1024)(128)(2,1)S(1)}) all-reduce(bf16[704]{0:T(1024)(128)(2,1)S(1)} %get-tuple-element.64, bf16[704]{0:T(1024)(128)(2,1)S(1)} %reduce_sum.567, bf16[704]{0:T(1024)(128)(2,1)S(1)} %get-tuple-element.124), channel_id=1, replica_groups=mesh['dp'=8,'chan'=4] {'dp'}, use_global_device_ids=true, to_apply=%region_61.62 | all-reduce | flops 2112 | bytes 8448 | tf_op jit(solution)/shard_map/psum | solution.py:124
  629.8 0.6 convert_element_type.85
  630.4 0.6 convert_element_type.86
  631.0 0.6 convert_element_type.91
  631.6 12.3 %fusion.102 = bf16[2,16,16,704]{3,2,1,0:T(8,128)(2,1)} fusion(f32[2,16,16,704]{3,2,1,0:T(8,128)S(1)} %bitcast.82, f32[704]{0:T(1024)S(1)} %get-tuple-element.115, f32[704]{0:T(1024)S(1)} %get-tuple-element.116, f32[704]{0:T(1024)S(1)} %get-tuple-element.69, f32[704]{0:T(1024)S(1)} %get-tuple-element.70, f32[704]{0:T(1024)S(1)} %get-tuple-element.71, ...), kind=kLoop, calls=%fused_computation.210 | loop fusion | flops 36044800 | bytes 3021568 | tf_op jit(solution)/shard_map/convert_element_type | solution.py:121
  643.9 1.6 convert_element_type.83
  645.5 152.7 %reduce-scatter.11.cloned.1.call-done = bf16[352,2816]{1,0:T(8,128)(2,1)} async-done(((bf16[2816,2816]{1,0:T(8,128)(2,1)}), bf16[352,2816]{1,0:T(8,128)(2,1)}) %reduce-scatter.11.cloned.1.call-update) | async-done | bytes 1982480 | tf_op jit(solution)/shard_map/reduce_scatter | solution.py:79
  798.2 3.7 convert_bitcast_fusion
  801.9 156.8 %reduce-scatter.9.cloned.1.call-done = bf16[352,2816]{1,0:T(8,128)(2,1)} async-done(((bf16[2816,2816]{1,0:T(8,128)(2,1)}), bf16[352,2816]{1,0:T(8,128)(2,1)}) %reduce-scatter.9.cloned.1.call-update) | async-done | bytes 1982480 | tf_op jit(solution)/shard_map/reduce_scatter | solution.py:63
  958.7 3.7 convert_element_type.88
  (84 shorter events, 0.7 us)
Async XLA Ops:
  7.2 82.8 %all-gather.5.cloned.1.call-start = ((), (), s32[]{:S(2)}) async-start(), calls=%async_computation.4 | async-start | bytes 3604480 | tf_op jit(solution)/shard_map/all_gather | solution.py:42
  24.8 19.9 %copy-start = (f32[2,16,16,704]{3,2,1,0:T(8,128)}, f32[2,16,16,704]{3,2,1,0:T(8,128)S(1)}, u32[]{:S(2)}) copy-start(f32[2,16,16,704]{3,2,1,0:T(8,128)S(1)} %get-tuple-element.123) | copy-start | bytes 4325380
  36.6 9.9 %copy-start.4 = (f32[704]{0:T(1024)S(1)}, f32[704]{0:T(1024)}, u32[]{:S(2)}) copy-start(f32[704]{0:T(1024)} %param.10) | copy-start | bytes 8452
  36.6 9.9 %copy-start.5 = (f32[704]{0:T(1024)S(1)}, f32[704]{0:T(1024)}, u32[]{:S(2)}) copy-start(f32[704]{0:T(1024)} %param.11) | copy-start | bytes 8452
  47.7 187.5 %all-gather.7.cloned.1.call-start = ((), (), s32[]{:S(2)}) async-start(), calls=%async_computation.5 | async-start | bytes 17842176 | tf_op jit(solution)/shard_map/all_gather | solution.py:43
  48.5 330.3 %all-gather.9.cloned.1.call-start = ((), (), s32[]{:S(2)}) async-start(), calls=%async_computation.6 | async-start | bytes 17842176 | tf_op jit(solution)/shard_map/all_gather | solution.py:46
  49.2 386.0 %reduce-scatter.5.cloned.1.call-start = ((), (), s32[]{:S(2)}) async-start(), calls=%async_computation.7 | async-start | bytes 3604480 | tf_op jit(solution)/shard_map/reduce_scatter | solution.py:48
  395.1 85.6 %all-gather.11.cloned.1.call-start = ((), (), s32[]{:S(2)}) async-start(), calls=%async_computation.8 | async-start | bytes 3604480 | tf_op jit(solution)/shard_map/all_gather | solution.py:56
  397.6 37.6 %copy-start.6 = (f32[704]{0:T(1024)S(1)}, f32[704]{0:T(1024)}, u32[]{:S(2)}) copy-start(f32[704]{0:T(1024)} %param.14) | copy-start | bytes 8452
  438.8 114.5 %reduce-scatter.7.cloned.1.call-start = ((), (), s32[]{:S(2)}) async-start(), calls=%async_computation.9 | async-start | bytes 3604480 | tf_op jit(solution)/shard_map/reduce_scatter | solution.py:74
  496.8 1.6 copy-start.7
  511.4 132.5 %all-reduce.6.cloned.1.call-start = ((), (), s32[]{:S(2)}) async-start(), calls=%async_computation.10 | async-start | bytes 172032 | tf_op jit(solution)/shard_map/psum | solution.py:123
  582.2 0.6 copy-start.3
  582.9 215.3 %reduce-scatter.11.cloned.1.call-start = ((), (), s32[]{:S(2)}) async-start(), calls=%async_computation.12 | async-start | bytes 17842176 | tf_op jit(solution)/shard_map/reduce_scatter | solution.py:79
  598.4 360.3 %reduce-scatter.9.cloned.1.call-start = ((), (), s32[]{:S(2)}) async-start(), calls=%async_computation.11 | async-start | bytes 17842176 | tf_op jit(solution)/shard_map/reduce_scatter | solution.py:63
  612.6 2.4 copy-start.1
  612.6 19.0 %copy-start.2 = (bf16[2,16,16,704]{3,2,1,0:T(8,128)(2,1)S(1)}, bf16[2,16,16,704]{3,2,1,0:T(8,128)(2,1)}, u32[]{:S(2)}) copy-start(bf16[2,16,16,704]{3,2,1,0:T(8,128)(2,1)} %param.15) | copy-start | bytes 2162692
Sparse Core Ops, SparseCore 0:
  47.9 42.1 all-gather.4
  91.7 143.5 all-gather.6
  236.9 141.8 all-gather.8
  395.2 39.9 reduce-scatter.4
  438.9 41.7 all-gather.10
  511.5 41.7 reduce-scatter.6
  583.0 49.9 all-reduce.5
  635.5 162.6 reduce-scatter.10
  800.7 157.9 reduce-scatter.8
where the time goes:
time: 974 us; the launch traced here: 969 us
  waiting for transfers between devices  744 us (76%)
  matrix products  89.7 us (9%)
  other arithmetic  58.8 us (6%)
  blocking collectives  43 us (4%)
  local copies, waits for them, and re-layouts  17.3 us (2%)
  between operations  14.7 us (2%)
    reduce_scatter x1, waiting for transfers between devices, body(): lax.psum_scatter(lax.dot_general(columns, dpre, (((0,), (0,)), ((), ())),...  157 us
    reduce_scatter x1, waiting for transfers between devices, body(): lax.psum_scatter(lax.dot_general(columns, hidden, (((0,), (0,)), ((), ())...  153 us
    all_gather x1, waiting for transfers between devices, body(): expand_all = lax.all_gather(w_expand, 'dp', axis=0, tiled=True)  145 us
    all_gather x1, waiting for transfers between devices, body(): reduce_all = lax.all_gather(w_reduce, 'dp', axis=1, tiled=True)  128 us
    reduce_scatter x1, waiting for transfers between devices, body(): lax.psum_scatter(partial_normed.astype(jnp.bfloat16), 'chan', scatter_dim...  41.9 us
    all_gather x1, waiting for transfers between devices, body(): dbranch_all = lax.all_gather(dbranch, 'chan', axis=1, tiled=True)  41.4 us
    all_gather x1, waiting for transfers between devices, body(): normed_all = lax.all_gather(normed_output, 'chan', axis=1, tiled=True)  40.4 us
    reduce_scatter x1, waiting for transfers between devices, body(): lax.psum_scatter(partial_branch.astype(jnp.bfloat16), 'chan', scatter_dim...  36 us
  transfers between devices with their start and end apart: 9, of which 8 were waited for; matrix products, arithmetic and copies ran while one was open for 7% of the time, Pallas kernels for 0%

commit v1 on v0

--- a/solution.py
+++ b/solution.py
@@ -39,7 +39,24 @@
     inverse_deviation = lax.rsqrt(var + eps)
     standardized_input = centred_rows * inverse_deviation
     normed_output = (standardized_input * layernorm_gain + layernorm_bias).astype(jnp.bfloat16)
-    normed_all = lax.all_gather(normed_output, "chan", axis=1, tiled=True)
+    finding, m_next, arr_now = (
+        jax.lax.psum(1, "chan"),
+        jax.lax.axis_index("chan"),
+        normed_output.shape[1],
+    )
+    nodes = [(dev_i, (dev_i + 1) % finding) for dev_i in range(finding)]
+    normed_all = jnp.zeros(
+        (*normed_output.shape[:1], finding * arr_now, *normed_output.shape[1 + 1 :]),
+        normed_output.dtype,
+    )
+    carry_in = normed_output
+    for k in range(finding):
+        kept_arr = (m_next - k) % finding
+        normed_all = lax.dynamic_update_slice_in_dim(
+            normed_all, carry_in, kept_arr * arr_now, axis=1
+        )
+        if k < finding - 1:
+            carry_in = jax.lax.ppermute(carry_in, "chan", perm=nodes)
     expand_all = lax.all_gather(w_expand, "dp", axis=0, tiled=True)
     pre = jnp.dot(normed_all, expand_all, preferred_element_type=jnp.float32)
     hidden = (pre * normal_cdf(pre)).astype(jnp.bfloat16)

time: 974 us -> 895 us (0.919)
  waiting for transfers between devices: 744 us -> 658 us
    all_gather x1, waiting for transfers between devices: 145 us -> 58.6 us  [body(): expand_all = lax.all_gather(w_expand, 'dp', axis=0, tiled=True)]
    ppermute x0 -> x3, waiting for transfers between devices: none -> 40.9 us  [body(): carry_in = jax.lax.ppermute(carry_in, 'chan', perm=nodes)]
    all_gather x1 -> x0, waiting for transfers between devices: 40.4 us -> none  [body(): normed_all = lax.all_gather(normed_output, 'chan', axis=1, tiled=True)]
  transfers between devices with their start and end apart: 9 -> 11, of which waited for: 8 -> 10; matrix products, arithmetic and copies ran while one was open for 7% -> 11% of each run, Pallas kernels for 0% -> 0%
where the time goes in v1:
time: 895 us; the launch traced here: 890 us
  waiting for transfers between devices  658 us (74%)
  matrix products  89.7 us (10%)
  other arithmetic  57.7 us (6%)
  blocking collectives  43 us (5%)
  local copies, waits for them, and re-layouts  23.1 us (3%)
  between operations  15.1 us (2%)
    reduce_scatter x1, waiting for transfers between devices, body(): lax.psum_scatter(lax.dot_general(columns, dpre, (((0,), (0,)), ((), ())),...  157 us
    reduce_scatter x1, waiting for transfers between devices, body(): lax.psum_scatter(lax.dot_general(columns, hidden, (((0,), (0,)), ((), ())...  153 us
    all_gather x1, waiting for transfers between devices, body(): reduce_all = lax.all_gather(w_reduce, 'dp', axis=1, tiled=True)  128 us
    all_gather x1, waiting for transfers between devices, body(): expand_all = lax.all_gather(w_expand, 'dp', axis=0, tiled=True)  58.6 us
    reduce_scatter x1, waiting for transfers between devices, body(): lax.psum_scatter(partial_normed.astype(jnp.bfloat16), 'chan', scatter_dim...  41.9 us
    all_gather x1, waiting for transfers between devices, body(): dbranch_all = lax.all_gather(dbranch, 'chan', axis=1, tiled=True)  41.4 us
    ppermute x3, waiting for transfers between devices, body(): carry_in = jax.lax.ppermute(carry_in, 'chan', perm=nodes)  40.9 us
    reduce_scatter x1, waiting for transfers between devices, body(): lax.psum_scatter(partial_branch.astype(jnp.bfloat16), 'chan', scatter_dim...  36 us
  transfers between devices with their start and end apart: 11, of which 10 were waited for; matrix products, arithmetic and copies ran while one was open for 11% of the time, Pallas kernels for 0%

profile of v1, /device:TPU:0, one launch (start us, length us, event | category | flops | bytes accessed | tf_op | source)
XLA Modules:
  0.0 890.3 jit_solution(8187435653636099195)
XLA Ops:
  7.2 0.7 all-gather.4.cloned.1.call-update
  8.0 0.7 all-gather.6.cloned.1.call-update
  8.7 0.2 convert_element_type.71
  8.9 0.7 copy-done.5
  9.6 0.1 slice_reduce_fusion.46
  9.7 0.2 slice_reduce_fusion.48
  9.8 0.2 slice_reduce_fusion.47
  10.0 12.3 %fusion.114 = (f32[2,16,16]{2,1,0:T(8,128)S(1)}, f32[2,16,16,704]{3,2,1,0:T(8,128)S(1)}) fusion(f32[704]{0:T(1024)S(1)} %get-tuple-element.115, f32[704]{0:T(1024)S(1)} %get-tuple-element.116, f32[704]{0:T(1024)S(1)} %get-tuple-element.69, f32[704]{0:T(1024)S(1)} %get-tuple-element.70, f32[704]{0:T(1024)S(1)} %get-tuple-element.71, ...), kind=kLoop, calls=%fused_computation.340 | loop fusion | flops 35323392 | bytes 3023616 | tf_op jit(solution)/shard_map/reduce_sum | solution.py:36
  22.3 0.1 reduce_sum.512
  22.4 11.3 %psum.56 = f32[512]{0:T(512)S(1)} all-reduce(f32[512]{0:T(512)S(1)} %reduce_sum.512), channel_id=1, replica_groups=mesh['dp'=8,'chan'=4] {'chan'}, use_global_device_ids=true, to_apply=%region_1.2 | all-reduce | flops 512 | bytes 4096 | tf_op jit(solution)/shard_map/psum | solution.py:36
  33.8 0.1 sub.37
  33.9 0.3 multiply_reduce_fusion.49
  34.2 0.1 reduce_sum.514
  34.2 1.9 copy.71
  36.1 8.0 psum.57
  44.1 1.8 broadcast_in_dim.2
  45.9 1.1 constant_dynamic-update-slice_fusion.10
  47.1 1.5 collective-permute-start
  48.5 14.9 %collective-permute-done = bf16[512,704]{0,1:T(8,128)(2,1)S(1)} collective-permute-done((bf16[512,704]{0,1:T(8,128)(2,1)S(1)}, bf16[512,704]{0,1:T(8,128)(2,1)S(1)}, u32[]{:S(2)}, u32[]{:S(2)}) %collective-permute-start) | collective-permute-done | bytes 720928 | tf_op jit(solution)/shard_map/ppermute | solution.py:59
  63.4 0.9 copy-done.4
  64.2 0.6 collective-permute-start.1
  64.8 15.3 %collective-permute-done.1 = bf16[512,704]{0,1:T(8,128)(2,1)} collective-permute-done((bf16[512,704]{0,1:T(8,128)(2,1)S(1)}, bf16[512,704]{0,1:T(8,128)(2,1)}, u32[]{:S(2)}, u32[]{:S(2)}) %collective-permute-start.1) | collective-permute-done | bytes 720928 | tf_op jit(solution)/shard_map/ppermute | solution.py:59
  80.1 0.3 collective-permute-start.2
  80.4 2.1 constant_dynamic-update-slice_fusion.9
  82.5 2.0 constant_dynamic-update-slice_fusion.8
  84.5 10.8 %collective-permute-done.2 = bf16[512,704]{0,1:T(8,128)(2,1)} collective-permute-done((bf16[512,704]{0,1:T(8,128)(2,1)}, bf16[512,704]{0,1:T(8,128)(2,1)}, u32[]{:S(2)}, u32[]{:S(2)}) %collective-permute-start.2) | collective-permute-done | bytes 720928 | tf_op jit(solution)/shard_map/ppermute | solution.py:59
  95.3 2.0 constant_dynamic-update-slice_fusion.7
  97.3 58.6 %all-gather.4.cloned.1.call-done = bf16[2816,2816]{1,0:T(8,128)(2,1)} async-done(((bf16[352,2816]{1,0:T(8,128)(2,1)}), bf16[2816,2816]{1,0:T(8,128)(2,1)}) %all-gather.4.cloned.1.call-update) | async-done | bytes 15859728 | tf_op jit(solution)/shard_map/all_gather | solution.py:60
  156.0 15.1 %fusion.115 = f32[512,2816]{1,0:T(8,128)} fusion(bf16[512,2816]{0,1:T(8,128)(2,1)} %constant_dynamic-update-slice_fusion.7, bf16[2816,2816]{1,0:T(8,128)(2,1)} %all-gather.4.cloned.1.call-done), kind=kOutput, calls=%fused_computation.341 | convolution fusion | flops 8120172544 | bytes 24510464 | tf_op jit(solution)/shard_map/dot_general | solution.py:61
  171.1 128.5 %all-gather.6.cloned.1.call-done = bf16[2816,2816]{0,1:T(8,128)(2,1)} async-done(((bf16[2816,352]{0,1:T(8,128)(2,1)}), bf16[2816,2816]{0,1:T(8,128)(2,1)}) %all-gather.6.cloned.1.call-update) | async-done | bytes 15859728 | tf_op jit(solution)/shard_map/all_gather | solution.py:63
  299.5 16.3 %convolution_convert_fusion.3 = bf16[512,2816]{0,1:T(8,128)(2,1)} fusion(bf16[2816,2816]{0,1:T(8,128)(2,1)} %all-gather.6.cloned.1.call-done, f32[512,2816]{1,0:T(8,128)} %fusion.115), kind=kOutput, calls=%fused_computation.108 | convolution fusion | flops 8128823296 | bytes 24510464 | tf_op jit(solution)/shard_map/dot_general | solution.py:64
  315.8 2.5 copy.74
  318.3 1.6 copy.72
  319.9 36.0 %reduce-scatter.5.cloned.1.call-done = bf16[512,704]{0,1:T(8,128)(2,1)} async-done(((bf16[512,2816]{0,1:T(8,128)(2,1)}), bf16[512,704]{0,1:T(8,128)(2,1)}) %reduce-scatter.5.cloned.1.call-update) | async-done | bytes 720912 | tf_op jit(solution)/shard_map/reduce_scatter | solution.py:65
  355.9 3.5 fusion.109
  359.5 0.6 reduce-scatter.7.cloned.1.call-start
  360.1 41.4 %all-gather.8.cloned.1.call-done = bf16[512,2816]{0,1:T(8,128)(2,1)} async-done(((bf16[512,704]{0,1:T(8,128)(2,1)}), bf16[512,2816]{0,1:T(8,128)(2,1)}) %all-gather.8.cloned.1.call-update) | async-done | bytes 2883600 | tf_op jit(solution)/shard_map/all_gather | solution.py:73
  401.4 16.0 %fusion.5 = bf16[512,2816]{1,0:T(8,128)(2,1)S(1)} fusion(f32[512,2816]{1,0:T(8,128)} %fusion.115, bf16[512,2816]{0,1:T(8,128)(2,1)} %all-gather.8.cloned.1.call-done, bf16[2816,2816]{0,1:T(8,128)(2,1)} %all-gather.6.cloned.1.call-done), kind=kOutput, calls=%fused_computation.104 | convolution fusion | flops 8134590464 | bytes 27394048 | tf_op jit(solution)/shard_map/dot_general | solution.py:74
  417.5 1.6 copy-done.10
  419.1 13.0 %convolution_convert_fusion.2 = bf16[512,2816]{0,1:T(8,128)(2,1)} fusion(bf16[512,2816]{1,0:T(8,128)(2,1)S(1)} %fusion.5, bf16[2816,2816]{1,0:T(8,128)(2,1)} %all-gather.4.cloned.1.call-done), kind=kOutput, calls=%fused_computation.107 | convolution fusion | flops 8121614336 | bytes 21626880 | tf_op jit(solution)/shard_map/dot_general | solution.py:88
  432.2 41.9 %reduce-scatter.7.cloned.1.call-done = bf16[512,704]{0,1:T(8,128)(2,1)} async-done(((bf16[512,2816]{0,1:T(8,128)(2,1)}), bf16[512,704]{0,1:T(8,128)(2,1)}) %reduce-scatter.7.cloned.1.call-update) | async-done | bytes 720912 | tf_op jit(solution)/shard_map/reduce_scatter | solution.py:91
  474.1 1.7 fusion.113
  475.8 9.1 %all-reduce.2 = (f32[512]{0:T(512)S(1)}, f32[512]{0:T(512)S(1)}) all-reduce(f32[512]{0:T(512)S(1)} %get-tuple-element.65, f32[512]{0:T(512)S(1)} %get-tuple-element.67), channel_id=1, replica_groups=mesh['dp'=8,'chan'=4] {'chan'}, use_global_device_ids=true, to_apply=%region_9.10 | all-reduce | flops 1024 | bytes 8192 | tf_op jit(solution)/shard_map/psum | solution.py:110
  484.9 2.6 fusion.111
  487.5 1.8 copy.75
  489.4 3.8 multiply_reduce_fusion.2
  493.2 4.2 multiply_reduce_fusion
  497.4 4.5 multiply_reduce_fusion.1
  503.0 0.6 copy-done.6
  503.7 15.4 %convolution_convert_fusion = bf16[2816,2816]{1,0:T(8,128)(2,1)} fusion(bf16[512,2816]{0,1:T(8,128)(2,1)} %all-gather.8.cloned.1.call-done, f32[512,2816]{1,0:T(8,128)} %fusion.115), kind=kOutput, calls=%fused_computation.96 | convolution fusion | flops 8135311360 | bytes 24510464 | tf_op jit(solution)/shard_map/dot_general | solution.py:97
  519.1 0.3 reduce-scatter.9.cloned.1.call-start
  519.4 13.9 %convolution_convert_fusion.1 = bf16[2816,2816]{1,0:T(8,128)(2,1)} fusion(bf16[512,2816]{0,1:T(8,128)(2,1)} %constant_dynamic-update-slice_fusion.7, bf16[512,2816]{1,0:T(8,128)(2,1)} %copy-done.10), kind=kOutput, calls=%fused_computation.97 | convolution fusion | flops 8128102400 | bytes 21626880 | tf_op jit(solution)/shard_map/dot_general | solution.py:81
  533.3 2.4 copy.73
  535.7 0.2 reduce_sum.567
  535.9 14.6 %all-reduce.3 = (bf16[704]{0:T(1024)(128)(2,1)S(1)}, bf16[704]{0:T(1024)(128)(2,1)S(1)}, bf16[704]{0:T(1024)(128)(2,1)S(1)}) all-reduce(bf16[704]{0:T(1024)(128)(2,1)S(1)} %get-tuple-element.64, bf16[704]{0:T(1024)(128)(2,1)S(1)} %reduce_sum.567, bf16[704]{0:T(1024)(128)(2,1)S(1)} %get-tuple-element.126), channel_id=1, replica_groups=mesh['dp'=8,'chan'=4] {'dp'}, use_global_device_ids=true, to_apply=%region_61.62 | all-reduce | flops 2112 | bytes 8448 | tf_op jit(solution)/shard_map/psum | solution.py:141
  550.5 0.6 convert_element_type.85
  551.1 0.6 convert_element_type.86
  551.7 0.6 convert_element_type.91
  552.3 12.3 %fusion.102 = bf16[2,16,16,704]{3,2,1,0:T(8,128)(2,1)} fusion(f32[2,16,16,704]{3,2,1,0:T(8,128)S(1)} %bitcast.82, f32[704]{0:T(1024)S(1)} %get-tuple-element.115, f32[704]{0:T(1024)S(1)} %get-tuple-element.116, f32[704]{0:T(1024)S(1)} %get-tuple-element.69, f32[704]{0:T(1024)S(1)} %get-tuple-element.70, f32[704]{0:T(1024)S(1)} %get-tuple-element.71, ...), kind=kLoop, calls=%fused_computation.210 | loop fusion | flops 36044800 | bytes 3021568 | tf_op jit(solution)/shard_map/convert_element_type | solution.py:138
  564.6 1.6 convert_element_type.83
  566.2 152.7 %reduce-scatter.11.cloned.1.call-done = bf16[352,2816]{1,0:T(8,128)(2,1)} async-done(((bf16[2816,2816]{1,0:T(8,128)(2,1)}), bf16[352,2816]{1,0:T(8,128)(2,1)}) %reduce-scatter.11.cloned.1.call-update) | async-done | bytes 1982480 | tf_op jit(solution)/shard_map/reduce_scatter | solution.py:96
  719.0 3.7 convert_bitcast_fusion
  722.7 156.7 %reduce-scatter.9.cloned.1.call-done = bf16[352,2816]{1,0:T(8,128)(2,1)} async-done(((bf16[2816,2816]{1,0:T(8,128)(2,1)}), bf16[352,2816]{1,0:T(8,128)(2,1)}) %reduce-scatter.9.cloned.1.call-update) | async-done | bytes 1982480 | tf_op jit(solution)/shard_map/reduce_scatter | solution.py:80
  879.5 3.7 convert_element_type.88
  (97 shorter events, 1.0 us)
Async XLA Ops:
  7.2 1.6 copy-start.2
  7.2 148.8 %all-gather.4.cloned.1.call-start = ((), (), s32[]{:S(2)}) async-start(), calls=%async_computation.4 | async-start | bytes 17842176 | tf_op jit(solution)/shard_map/all_gather | solution.py:60
  7.9 291.6 %all-gather.6.cloned.1.call-start = ((), (), s32[]{:S(2)}) async-start(), calls=%async_computation.5 | async-start | bytes 17842176 | tf_op jit(solution)/shard_map/all_gather | solution.py:63
  8.7 0.9 copy-start.5
  8.7 347.3 %reduce-scatter.5.cloned.1.call-start = ((), (), s32[]{:S(2)}) async-start(), calls=%async_computation.6 | async-start | bytes 3604480 | tf_op jit(solution)/shard_map/reduce_scatter | solution.py:65
  22.3 11.9 %copy-start = (f32[2,16,16,704]{3,2,1,0:T(8,128)}, f32[2,16,16,704]{3,2,1,0:T(8,128)S(1)}, u32[]{:S(2)}) copy-start(f32[2,16,16,704]{3,2,1,0:T(8,128)S(1)} %get-tuple-element.125) | copy-start | bytes 4325380
  36.1 9.8 %copy-start.7 = (f32[704]{0:T(1024)S(1)}, f32[704]{0:T(1024)}, u32[]{:S(2)}) copy-start(f32[704]{0:T(1024)} %param.10) | copy-start | bytes 8452
  36.1 9.8 %copy-start.8 = (f32[704]{0:T(1024)S(1)}, f32[704]{0:T(1024)}, u32[]{:S(2)}) copy-start(f32[704]{0:T(1024)} %param.11) | copy-start | bytes 8452
  47.1 16.3 %collective-permute-start = (bf16[512,704]{0,1:T(8,128)(2,1)S(1)}, bf16[512,704]{0,1:T(8,128)(2,1)S(1)}, u32[]{:S(2)}, u32[]{:S(2)}) collective-permute-start(bf16[512,704]{0,1:T(8,128)(2,1)S(1)} %get-tuple-element.123), channel_id=1, source_target_pairs={{0,1},{1,2},{2,3},{3,0},{4,5},{5,6},{6,7},{7,4},{8,9},{9,10},{10,1... | collective-permute-start | bytes 2162696 | tf_op jit(solution)/shard_map/ppermute | solution.py:59
  63.4 0.9 copy-start.4
  64.2 15.8 %collective-permute-start.1 = (bf16[512,704]{0,1:T(8,128)(2,1)S(1)}, bf16[512,704]{0,1:T(8,128)(2,1)}, u32[]{:S(2)}, u32[]{:S(2)}) collective-permute-start(bf16[512,704]{0,1:T(8,128)(2,1)S(1)} %collective-permute-done), channel_id=1, source_target_pairs={{0,1},{1,2},{2,3},{3,0},{4,5},{5,6},{6,7},{7,4},{8,9},{9,10},{10,1... | collective-permute-start | bytes 2162696 | tf_op jit(solution)/shard_map/ppermute | solution.py:59
  80.1 15.3 %collective-permute-start.2 = (bf16[512,704]{0,1:T(8,128)(2,1)}, bf16[512,704]{0,1:T(8,128)(2,1)}, u32[]{:S(2)}, u32[]{:S(2)}) collective-permute-start(bf16[512,704]{0,1:T(8,128)(2,1)} %collective-permute-done.1), channel_id=1, source_target_pairs={{0,1},{1,2},{2,3},{3,0},{4,5},{5,6},{6,7},{7,4},{8,9},{9,10},{10,1... | collective-permute-start | bytes 2162696 | tf_op jit(solution)/shard_map/ppermute | solution.py:59
  315.8 85.6 %all-gather.8.cloned.1.call-start = ((), (), s32[]{:S(2)}) async-start(), calls=%async_computation.7 | async-start | bytes 3604480 | tf_op jit(solution)/shard_map/all_gather | solution.py:73
  318.3 37.6 %copy-start.9 = (f32[704]{0:T(1024)S(1)}, f32[704]{0:T(1024)}, u32[]{:S(2)}) copy-start(f32[704]{0:T(1024)} %param.14) | copy-start | bytes 8452
  359.5 114.6 %reduce-scatter.7.cloned.1.call-start = ((), (), s32[]{:S(2)}) async-start(), calls=%async_computation.8 | async-start | bytes 3604480 | tf_op jit(solution)/shard_map/reduce_scatter | solution.py:91
  417.5 1.6 copy-start.10
  432.2 132.5 %all-reduce.6.cloned.1.call-start = ((), (), s32[]{:S(2)}) async-start(), calls=%async_computation.9 | async-start | bytes 172032 | tf_op jit(solution)/shard_map/psum | solution.py:140
  503.0 0.6 copy-start.6
  503.6 215.3 %reduce-scatter.11.cloned.1.call-start = ((), (), s32[]{:S(2)}) async-start(), calls=%async_computation.11 | async-start | bytes 17842176 | tf_op jit(solution)/shard_map/reduce_scatter | solution.py:96
  519.1 360.3 %reduce-scatter.9.cloned.1.call-start = ((), (), s32[]{:S(2)}) async-start(), calls=%async_computation.10 | async-start | bytes 17842176 | tf_op jit(solution)/shard_map/reduce_scatter | solution.py:80
  533.3 2.4 copy-start.1
  533.3 19.0 %copy-start.3 = (bf16[2,16,16,704]{3,2,1,0:T(8,128)(2,1)S(1)}, bf16[2,16,16,704]{3,2,1,0:T(8,128)(2,1)}, u32[]{:S(2)}) copy-start(bf16[2,16,16,704]{3,2,1,0:T(8,128)(2,1)} %param.15) | copy-start | bytes 2162692
Sparse Core Ops, SparseCore 0:
  9.7 146.2 all-gather.3
  157.6 141.8 all-gather.5
  315.9 39.9 reduce-scatter.4
  359.6 41.7 all-gather.7
  432.3 41.7 reduce-scatter.6
  503.8 49.9 all-reduce.5
  556.3 162.6 reduce-scatter.10
  721.4 157.9 reduce-scatter.8
